TPU v7x, 32 devices: a whole 2x2x4 slice. The times are simulated.
32 devices in a mesh: tm: 4 (over y, x), op: 8 (over z, core).
Axes of the slice: x: 2, y: 2, z: 4, core: 2. Of those that a mesh axis runs over, the one named last changes fastest.
Arguments:
- sink_elem: bfloat16 [2, 4, 2048, 16384], P(None, 'tm', 'op'), may hold values from -6 to 6
- source_elem: bfloat16 [2, 2, 2048, 16384], P(None, None, None, 'op'), may hold values from -6 to 6
- peram: bfloat16 [2, 4, 2, 512, 512], P(None, 'tm', None, 'op'), may hold values from -4 to 4
- pair_list: int32 [16, 1], replicated, may hold values from 0 to 15
- spin_sets: int32 [16, 3], replicated, may hold values from 0 to 3
Outputs:
- correlator: float32 [2, 4, 2, 16, 1], P(None, 'tm')
All inputs are finite; a program needn't handle non-finite values.
Results may differ from a plain program's by a relative error of at most 0.0041.
Values may be sent and summed in bfloat16 or wider, within the bound.
No kernel may reach another device: no remote copies, remote signals or barrier semaphores. Data moves between devices by JAX's collectives and lax.ppermute only.
A program may use at most 256 MiB of HBM per device.

v0:
```python
import jax
import jax.numpy as jnp
from jax import lax
from jax.sharding import PartitionSpec as P

NEV = 128
NSPIN = 4
NOP = 16
TSRC = 2
PAIRS = 1


def complex_matrix(block):
    upper = jnp.concatenate([block[0], block[1]], axis=1)
    lower = jnp.concatenate([-block[1], block[0]], axis=1)
    return jnp.stack([upper, lower])


def on_device(sink_elem, source_elem, peram, pair_list, spin_sets):
    tau_all = lax.all_gather(peram, "op", axis=3, tiled=True)
    position = lax.axis_index("op")
    rows = sink_elem.shape[2]
    local_times = sink_elem.shape[1]
    span = min(rows, NEV)
    groups = rows // span
    cols = source_elem.shape[3]

    def spin_block(local, t0, left, right):
        return lax.dynamic_slice(tau_all[:, local, t0], (0, left * NEV, right * NEV), (2, NEV, NEV))

    def sink_side(local, t0, p):
        pieces = []
        for group in range(groups):
            op_now = (position * rows + group * span) // NEV
            mine = spin_sets[op_now]
            theirs = spin_sets[pair_list[op_now, p]]
            third = complex_matrix(spin_block(local, t0, mine[2], theirs[2]))
            second = complex_matrix(spin_block(local, t0, mine[1], theirs[1]))
            phi = sink_elem[:, local, group * span : (group + 1) * span].reshape(2, span * NEV, NEV)
            x_both = jnp.einsum("cxk,ckb->xb", phi, third, preferred_element_type=jnp.float32)
            x_both = x_both.astype(jnp.bfloat16).reshape(span, NEV, 2, NEV)
            y_both = jnp.einsum("ijck,cjb->ibk", x_both, second, preferred_element_type=jnp.float32)
            y_both = y_both.astype(jnp.bfloat16).reshape(span, 2, NEV * NEV)
            pieces.append(jnp.transpose(y_both, (1, 0, 2)))
        return jnp.concatenate(pieces, axis=1)

    partial_terms = {}
    for t0 in range(TSRC):
        combos = [(local, t0, p) for local in range(local_times) for p in range(PAIRS)]
        stacked = jnp.stack([sink_side(local, t0, p) for local, t0, p in combos], axis=1)
        columns = lax.all_to_all(stacked, "op", split_axis=3, concat_axis=2, tiled=True)
        for index, combo in enumerate(combos):
            column_t0 = combo[1]
            other = pair_list[:, combo[2]]
            source = source_elem[:, column_t0].reshape(2, NOP, NEV, cols)
            chosen = jnp.take(source, other, axis=1)
            tiles = columns[:, index].reshape(2, NOP, NEV, cols)

            def inner(a, b):
                return jnp.einsum("oic,ojc->oij", a, b, preferred_element_type=jnp.float32)

            m_re = inner(tiles[0], chosen[0]) + inner(tiles[1], chosen[1])
            m_im = inner(tiles[1], chosen[0]) - inner(tiles[0], chosen[1])
            blocks = tau_all[:, combo[0], column_t0].reshape(2, NSPIN, NEV, NSPIN, NEV)
            blocks = jnp.transpose(blocks, (1, 3, 0, 2, 4))
            first = blocks[spin_sets[:, 0], spin_sets[other, 0]].astype(jnp.float32)
            c_re = jnp.sum(first[:, 0] * m_re - first[:, 1] * m_im, axis=(1, 2))
            c_im = jnp.sum(first[:, 0] * m_im + first[:, 1] * m_re, axis=(1, 2))
            partial_terms[combo] = jnp.stack([c_re, c_im])
    local = 0
    per_time = []
    for t0 in range(TSRC):
        per_time.append(jnp.stack([partial_terms[local, t0, 0]], axis=-1))
    per_local = [jnp.stack(per_time, axis=1)]
    partial_sum = jnp.stack(per_local, axis=1)
    totals = lax.psum(partial_sum, "op")
    return totals * (1.0 / float(NEV**3))


def solution(mesh):
    in_specs = (
        P(None, "tm", "op", None),
        P(None, None, None, "op"),
        P(None, "tm", None, "op", None),
        P(),
        P(),
    )
    out_specs = P(None, "tm", None, None, None)
    return jax.shard_map(
        on_device, mesh=mesh, in_specs=in_specs, out_specs=out_specs, check_vma=False
    )
```

profile of v0, /device:TPU:0, one launch (start us, length us, event | category | flops | bytes accessed | tf_op | source)
XLA Modules:
  0.0 1121.4 jit_solution(15769526317778974320)
XLA Ops:
  20.9 11.6 %fusion.86 = (bf16[2,1,128,16384]{3,2,1,0:T(8,128)(2,1)}, bf16[2,1,128,16384]{3,2,1,0:T(8,128)(2,1)}) fusion(bf16[2,1,256,16384]{3,2,1,0:T(8,128)(2,1)} %param.7), kind=kLoop, calls=%fused_computation.166 | loop fusion | bytes 33554432 | tf_op jit(solution)/shard_map/slice | solution.py:39
  32.5 13.5 %reshape_squeeze.23 = bf16[2,16384,128]{2,1,0:T(8,128)(2,1)} reshape(bf16[2,1,128,16384]{3,2,1,0:T(8,128)(2,1)} %get-tuple-element.32) | data formatting | bytes 16777216 | tf_op jit(solution)/shard_map/reshape;squeeze | solution.py:39
  45.9 13.5 %reshape_squeeze.24 = bf16[2,16384,128]{2,1,0:T(8,128)(2,1)} reshape(bf16[2,1,128,16384]{3,2,1,0:T(8,128)(2,1)} %get-tuple-element.33) | data formatting | bytes 16777216 | tf_op jit(solution)/shard_map/reshape;squeeze | solution.py:39
  89.1 26.0 %fusion.18 = bf16[128,256,128]{2,1,0:T(8,128)(2,1)} fusion(bf16[128,128,2,128]{1,0,3,2:T(8,128)(2,1)} %bitcast.312, bf16[1,128,256]{1,2,0:T(8,128)(2,1)S(1)} %get-tuple-element.57, bf16[1,128,256]{1,2,0:T(8,128)(2,1)S(1)} %get-tuple-element.56), kind=kOutput, calls=%fused_computation.43 | convolution fusion | flops 2151940096 | bytes 16908288 | tf_op jit(solution)/shard_map/ijck,cjb->ibk/dot_general | solution.py:42
  115.1 12.7 %reshape.125 = bf16[128,2,16384]{2,1,0:T(2,128)(2,1)} reshape(bf16[128,256,128]{2,1,0:T(8,128)(2,1)} %fusion.18) | data formatting | bytes 16777216 | tf_op jit(solution)/shard_map/reshape | solution.py:43
  127.8 12.0 %copy.116 = bf16[128,2,16384]{2,0,1:T(8,128)(2,1)} copy(bf16[128,2,16384]{2,1,0:T(2,128)(2,1)} %reshape.125) | data formatting | bytes 16777216 | tf_op jit(solution)/shard_map/reshape | solution.py:43
  158.0 25.8 %fusion.21 = bf16[128,256,128]{2,1,0:T(8,128)(2,1)} fusion(bf16[128,128,2,128]{1,0,3,2:T(8,128)(2,1)} %bitcast.310, bf16[1,128,256]{1,2,0:T(8,128)(2,1)S(1)} %get-tuple-element.61, bf16[1,128,256]{1,2,0:T(8,128)(2,1)S(1)} %get-tuple-element.60), kind=kOutput, calls=%fused_computation.44 | convolution fusion | flops 2151940096 | bytes 16908288 | tf_op jit(solution)/shard_map/ijck,cjb->ibk/dot_general | solution.py:42
  183.8 12.9 %reshape.127 = bf16[128,2,16384]{2,1,0:T(2,128)(2,1)} reshape(bf16[128,256,128]{2,1,0:T(8,128)(2,1)} %fusion.21) | data formatting | bytes 16777216 | tf_op jit(solution)/shard_map/reshape | solution.py:43
  196.7 12.0 %copy.115 = bf16[128,2,16384]{2,0,1:T(8,128)(2,1)} copy(bf16[128,2,16384]{2,1,0:T(2,128)(2,1)} %reshape.127) | data formatting | bytes 16777216 | tf_op jit(solution)/shard_map/reshape | solution.py:43
  208.7 13.9 %pad_maximum_fusion = bf16[2,256,16384]{2,1,0:T(8,128)(2,1)} fusion(bf16[2,128,16384]{2,1,0:T(8,128)(2,1)} %bitcast.316, bf16[2,128,16384]{2,1,0:T(8,128)(2,1)} %bitcast.315), kind=kLoop, calls=%fused_computation.13 | loop fusion | flops 33554432 | bytes 33554432 | tf_op jit(solution)/shard_map/concatenate | solution.py:45
  222.5 40.8 %copy.59 = bf16[2,256,16384]{1,0,2:T(2,128)(2,1)} copy(bf16[2,256,16384]{2,1,0:T(8,128)(2,1)} %pad_maximum_fusion) | data formatting | bytes 33554432 | tf_op jit(solution)/shard_map/concatenate | solution.py:45
  290.7 25.8 %fusion.24 = bf16[128,256,128]{2,1,0:T(8,128)(2,1)} fusion(bf16[128,128,2,128]{1,0,3,2:T(8,128)(2,1)} %bitcast.313, bf16[1,128,256]{1,2,0:T(8,128)(2,1)S(1)} %get-tuple-element.65, bf16[1,128,256]{1,2,0:T(8,128)(2,1)S(1)} %get-tuple-element.64), kind=kOutput, calls=%fused_computation.45 | convolution fusion | flops 2151940096 | bytes 16908288 | tf_op jit(solution)/shard_map/ijck,cjb->ibk/dot_general | solution.py:42
  316.5 12.7 %reshape.129 = bf16[128,2,16384]{2,1,0:T(2,128)(2,1)} reshape(bf16[128,256,128]{2,1,0:T(8,128)(2,1)} %fusion.24) | data formatting | bytes 16777216 | tf_op jit(solution)/shard_map/reshape | solution.py:43
  329.2 12.0 %copy.114 = bf16[128,2,16384]{2,0,1:T(8,128)(2,1)} copy(bf16[128,2,16384]{2,1,0:T(2,128)(2,1)} %reshape.129) | data formatting | bytes 16777216 | tf_op jit(solution)/shard_map/reshape | solution.py:43
  359.4 25.8 %fusion.27 = bf16[128,256,128]{2,1,0:T(8,128)(2,1)} fusion(bf16[128,128,2,128]{1,0,3,2:T(8,128)(2,1)} %bitcast.311, bf16[1,128,256]{1,2,0:T(8,128)(2,1)S(1)} %get-tuple-element.69, bf16[1,128,256]{1,2,0:T(8,128)(2,1)S(1)} %get-tuple-element.68), kind=kOutput, calls=%fused_computation.46 | convolution fusion | flops 2151940096 | bytes 16908288 | tf_op jit(solution)/shard_map/ijck,cjb->ibk/dot_general | solution.py:42
  385.2 13.0 %reshape.131 = bf16[128,2,16384]{2,1,0:T(2,128)(2,1)} reshape(bf16[128,256,128]{2,1,0:T(8,128)(2,1)} %fusion.27) | data formatting | bytes 16777216 | tf_op jit(solution)/shard_map/reshape | solution.py:43
  398.2 12.0 %copy.113 = bf16[128,2,16384]{2,0,1:T(8,128)(2,1)} copy(bf16[128,2,16384]{2,1,0:T(2,128)(2,1)} %reshape.131) | data formatting | bytes 16777216 | tf_op jit(solution)/shard_map/reshape | solution.py:43
  410.1 13.8 %pad_maximum_fusion.1 = bf16[2,256,16384]{2,1,0:T(8,128)(2,1)} fusion(bf16[2,128,16384]{2,1,0:T(8,128)(2,1)} %bitcast.317, bf16[2,128,16384]{2,1,0:T(8,128)(2,1)} %bitcast.314), kind=kLoop, calls=%fused_computation.14 | loop fusion | flops 33554432 | bytes 33554432 | tf_op jit(solution)/shard_map/concatenate | solution.py:45
  424.0 40.7 %copy.69 = bf16[2,256,16384]{1,0,2:T(2,128)(2,1)} copy(bf16[2,256,16384]{2,1,0:T(8,128)(2,1)} %pad_maximum_fusion.1) | data formatting | bytes 33554432 | tf_op jit(solution)/shard_map/concatenate | solution.py:45
  464.7 168.9 %all-to-all-done = bf16[2,1,256,16384]{2,0,1,3:T(2,128)(2,1)} async-done(((bf16[2,1,256,16384]{2,0,1,3:T(2,128)(2,1)}), bf16[2,1,256,16384]{2,0,1,3:T(2,128)(2,1)}, u32[]{:S(2)}, u32[]{:S(2)}) %all-to-all-start) | async-done | bytes 16777248 | tf_op jit(solution)/shard_map/all_to_all | solution.py:51
  639.7 23.5 %fusion.83 = (bf16[2,1,2048,2048]{3,2,1,0:T(8,128)(2,1)}, bf16[2,1,2048,2048]{3,2,1,0:T(8,128)(2,1)}) fusion(bf16[2,2,2048,2048]{3,2,1,0:T(8,128)(2,1)} %param.8), kind=kLoop, calls=%fused_computation.163 | loop fusion | bytes 67108864 | tf_op jit(solution)/shard_map/slice | solution.py:55
  663.2 13.1 %gather_fusion.3 = bf16[16,2,128,2048]{3,2,1,0:T(8,128)(2,1)} fusion(bf16[2,16,128,2048]{3,2,1,0:T(8,128)(2,1)} %bitcast.309, s32[1024]{0:T(1024)S(1)} %pad_clamp_fusion), kind=kCustom, calls=%fused_computation.clone | custom fusion | bytes 33554496 | tf_op jit(solution)/shard_map/jit(_take)/gather | solution.py:56
  676.4 13.1 %gather_fusion.4 = bf16[16,2,128,2048]{3,2,1,0:T(8,128)(2,1)} fusion(bf16[2,16,128,2048]{3,2,1,0:T(8,128)(2,1)} %bitcast.308, s32[1024]{0:T(1024)S(1)} %pad_clamp_fusion), kind=kCustom, calls=%fused_computation.1.clone | custom fusion | bytes 33554496 | tf_op jit(solution)/shard_map/jit(_take)/gather | solution.py:56
  690.2 23.2 %fusion.5 = (bf16[2,16,128,2048]{3,2,1,0:T(8,128)(2,1)}, bf16[2,16,128,2048]{3,2,1,0:T(8,128)(2,1)}) fusion(bf16[16,2,128,2048]{3,2,1,0:T(8,128)(2,1)} %gather_fusion.3, pred[16]{0:T(512)(128)(4,1)S(1)} %compare_and_fusion, bf16[16,2,128,2048]{3,2,1,0:T(8,128)(2,1)} %gather_fusion.4), kind=kLoop, calls=%fused_computation.22 | loop fusion | flops 16777216 | bytes 67108880 | tf_op jit(solution)/shard_map/jit(_take)/select_n | solution.py:56
  722.0 41.0 %copy.60 = bf16[2,1,256,8,2048]{4,2,3,1,0:T(8,128)(2,1)} copy(bf16[2,1,256,8,2048]{2,0,4,3,1:T(2,128)(2,1)} %bitcast.46) | data formatting | bytes 33554432 | tf_op jit(solution)/shard_map/all_to_all | solution.py:51
  763.0 9.4 fusion.84
  772.4 12.2 %fusion.10 = f32[16,128,128]{2,1,0:T(8,128)} fusion(bf16[16,128,2048]{2,1,0:T(8,128)(2,1)} %bitcast.324, bf16[2,16,128,2048]{3,2,1,0:T(8,128)(2,1)} %get-tuple-element.84), kind=kOutput, calls=%fused_computation.35 | convolution fusion | flops 1073741824 | bytes 17825792 | tf_op jit(solution)/shard_map/oic,ojc->oij/dot_general | solution.py:60
  798.5 204.9 %all-to-all-done.1 = bf16[2,1,256,16384]{2,0,1,3:T(2,128)(2,1)} async-done(((bf16[2,1,256,16384]{2,0,1,3:T(2,128)(2,1)}), bf16[2,1,256,16384]{2,0,1,3:T(2,128)(2,1)}, u32[]{:S(2)}, u32[]{:S(2)}) %all-to-all-start.1) | async-done | bytes 16777248 | tf_op jit(solution)/shard_map/all_to_all | solution.py:51
  1003.3 41.0 %copy.70 = bf16[2,1,256,8,2048]{4,2,3,1,0:T(8,128)(2,1)} copy(bf16[2,1,256,8,2048]{2,0,4,3,1:T(2,128)(2,1)} %bitcast.92) | data formatting | bytes 33554432 | tf_op jit(solution)/shard_map/all_to_all | solution.py:51
  1044.3 9.6 fusion.85
  1053.9 12.1 %fusion.14 = f32[16,128,128]{2,1,0:T(8,128)} fusion(bf16[16,128,2048]{2,1,0:T(8,128)(2,1)} %bitcast.322, bf16[2,16,128,2048]{3,2,1,0:T(8,128)(2,1)} %get-tuple-element.85), kind=kOutput, calls=%fused_computation.39 | convolution fusion | flops 1073741824 | bytes 17825792 | tf_op jit(solution)/shard_map/oic,ojc->oij/dot_general | solution.py:60
  1099.2 14.5 %psum.7 = f32[2,1,2,16,1]{3,2,0,4,1:T(2,128)S(1)} all-reduce(f32[2,1,2,16,1]{3,2,0,4,1:T(2,128)S(1)} %bitcast.328), channel_id=1, replica_groups=mesh['tm'=4,'op'=8] {'op'}, use_global_device_ids=true, to_apply=%region_4.6 | all-reduce | flops 64 | bytes 512 | tf_op jit(solution)/shard_map/psum | solution.py:76
  (74 shorter events, 161.8 us)
Async XLA Ops:
  6.5 52.9 %all-gather.2.cloned.1.call-start = ((), (), s32[]{:S(2)}) async-start(), calls=%async_computation.2 | async-start | bytes 2359296 | tf_op jit(solution)/shard_map/all_gather | solution.py:20
  70.5 9.4 copy-start.3
  263.4 370.3 %all-to-all-start = ((bf16[2,1,256,16384]{2,0,1,3:T(2,128)(2,1)}), bf16[2,1,256,16384]{2,0,1,3:T(2,128)(2,1)}, u32[]{:S(2)}, u32[]{:S(2)}) async-start(bf16[2,1,256,16384]{2,0,1,3:T(2,128)(2,1)} %bitcast.304), calls=%async_computation | async-start | bytes 33554432 | tf_op jit(solution)/shard_map/all_to_all | solution.py:51
  633.6 6.1 copy-start.7
  633.7 369.7 %all-to-all-start.1 = ((bf16[2,1,256,16384]{2,0,1,3:T(2,128)(2,1)}), bf16[2,1,256,16384]{2,0,1,3:T(2,128)(2,1)}, u32[]{:S(2)}, u32[]{:S(2)}) async-start(bf16[2,1,256,16384]{2,0,1,3:T(2,128)(2,1)} %bitcast.305), calls=%async_computation.1 | async-start | bytes 33554432 | tf_op jit(solution)/shard_map/all_to_all | solution.py:51
  676.4 13.1 %copy-start = (s32[16,3]{0,1:T(4,128)S(1)}, s32[16,3]{0,1:T(4,128)}, u32[]{:S(2)}) copy-start(s32[16,3]{0,1:T(4,128)} %param.11) | copy-start | bytes 580
  690.1 23.2 %copy-start.4 = (bf16[2,1,1,512,512]{3,4,2,1,0:T(8,128)(2,1)S(1)}, bf16[2,1,1,512,512]{3,4,2,1,0:T(8,128)(2,1)}, u32[]{:S(2)}) copy-start(bf16[2,1,1,512,512]{3,4,2,1,0:T(8,128)(2,1)} %copy-done.3) | copy-start | bytes 3145732
  772.4 12.2 %copy-start.1 = (bf16[1,1,8,256,2048]{4,3,2,1,0:T(8,128)(2,1)}, bf16[1,1,8,256,2048]{4,3,2,1,0:T(8,128)(2,1)S(1)}, u32[]{:S(2)}) copy-start(bf16[1,1,8,256,2048]{4,3,2,1,0:T(8,128)(2,1)S(1)} %get-tuple-element.28) | copy-start | bytes 25165828
  1053.9 12.1 %copy-start.2 = (bf16[1,1,8,256,2048]{4,3,2,1,0:T(8,128)(2,1)}, bf16[1,1,8,256,2048]{4,3,2,1,0:T(8,128)(2,1)S(1)}, u32[]{:S(2)}) copy-start(bf16[1,1,8,256,2048]{4,3,2,1,0:T(8,128)(2,1)S(1)} %get-tuple-element.30) | copy-start | bytes 25165828
  1072.8 8.5 copy-start.6
  1081.3 9.0 copy-start.5
Sparse Core Ops, SparseCore 0:
  8.9 31.8 all-gather.1
where the time goes:
time: 1130 us; the launch traced here: 1120 us
  local copies, waits for them, and re-layouts  432 us (38%)
  waiting for transfers between devices  374 us (33%)
  matrix products  211 us (19%)
  other arithmetic  54.8 us (5%)
  between operations  22.9 us (2%)
  blocking collectives  14.5 us (1%)
  starting transfers between devices  12.5 us (1%)
    all_to_all x2, waiting for transfers between devices, on_device(): lax.all_to_all(stacked, 'op', split_axis=3, concat_axis=2, tiled=True)  374 us
    dot_general x4, matrix products, sink_side(): jnp.einsum('ijck,cjb->ibk', x_both, second, preferred_element_type=jnp.fl...  103 us
    reshape x8, local copies, waits for them, and re-layouts, sink_side(): y_both = y_both.astype(jnp.bfloat16).reshape(span, 2, NEV * NEV)  99.1 us
    all_to_all x2, local copies, waits for them, and re-layouts, on_device(): lax.all_to_all(stacked, 'op', split_axis=3, concat_axis=2, tiled=True)  82 us
    concatenate x2, local copies, waits for them, and re-layouts, sink_side(): return jnp.concatenate(pieces, axis=1)  81.6 us
    dot_general x8, matrix products, inner(): return jnp.einsum('oic,ojc->oij', a, b, preferred_element_type=jnp.float32)  71.2 us
    unnamed x23, local copies, waits for them, and re-layouts  45.9 us
    dot_general x4, matrix products, sink_side(): jnp.einsum('cxk,ckb->xb', phi, third, preferred_element_type=jnp.float32)  36.2 us
  transfers between devices with their start and end apart: 3, of which 2 were waited for; matrix products, arithmetic and copies ran while one was open for 35% of the time, Pallas kernels for 0%

commit v1 on v0

--- a/solution.py
+++ b/solution.py
@@ -48,7 +48,10 @@
     for t0 in range(TSRC):
         combos = [(local, t0, p) for local in range(local_times) for p in range(PAIRS)]
         stacked = jnp.stack([sink_side(local, t0, p) for local, t0, p in combos], axis=1)
-        columns = lax.all_to_all(stacked, "op", split_axis=3, concat_axis=2, tiled=True)
+        columns = jnp.concatenate(
+            lax.all_to_all(jnp.stack(jnp.split(stacked, lax.axis_size("op"), axis=3)), "op", 0, 0),
+            axis=2,
+        )
         for index, combo in enumerate(combos):
             column_t0 = combo[1]
             other = pair_list[:, combo[2]]

time: 1130 us -> 1060 us (0.938)
  local copies, waits for them, and re-layouts: 432 us -> 300 us
  waiting for transfers between devices: 374 us -> 445 us
    concatenate x2 -> x0, local copies, waits for them, and re-layouts: 81.6 us -> none  [sink_side(): return jnp.concatenate(pieces, axis=1)]
    all_to_all x2, waiting for transfers between devices: 374 us -> 445 us  [on_device(): lax.all_to_all(jnp.stack(jnp.split(stacked, lax.axis_size('op'), axis=3))...]
    all_to_all x2, local copies, waits for them, and re-layouts: 82 us -> 16.8 us  [on_device(): lax.all_to_all(jnp.stack(jnp.split(stacked, lax.axis_size('op'), axis=3))...]
    concatenate x2 -> x0, other arithmetic: 27.7 us -> none  [sink_side(): return jnp.concatenate(pieces, axis=1)]
    unnamed x23 -> x37, local copies, waits for them, and re-layouts: 45.9 us -> 68.1 us
    another operation x0 -> x2, other arithmetic: none -> 16.6 us  [on_device(): jnp.stack([sink_side(local, t0, p) for local, t0, p in combos], axis=1)]
  transfers between devices with their start and end apart: 3 -> 3, of which waited for: 2 -> 2; matrix products, arithmetic and copies ran while one was open for 35% -> 31% of each run, Pallas kernels for 0% -> 0%
where the time goes in v1:
time: 1060 us; the launch traced here: 1050 us
  waiting for transfers between devices  445 us (42%)
  local copies, waits for them, and re-layouts  300 us (28%)
  matrix products  211 us (20%)
  other arithmetic  43.7 us (4%)
  between operations  23.1 us (2%)
  blocking collectives  14.5 us (1%)
  starting transfers between devices  12.3 us (1%)
    all_to_all x2, waiting for transfers between devices, on_device(): lax.all_to_all(jnp.stack(jnp.split(stacked, lax.axis_size('op'), axis=3))...  445 us
    dot_general x4, matrix products, sink_side(): jnp.einsum('ijck,cjb->ibk', x_both, second, preferred_element_type=jnp.fl...  104 us
    reshape x8, local copies, waits for them, and re-layouts, sink_side(): y_both = y_both.astype(jnp.bfloat16).reshape(span, 2, NEV * NEV)  98.8 us
    dot_general x8, matrix products, inner(): return jnp.einsum('oic,ojc->oij', a, b, preferred_element_type=jnp.float32)  71.1 us
    unnamed x37, local copies, waits for them, and re-layouts  68.1 us
    dot_general x4, matrix products, sink_side(): jnp.einsum('cxk,ckb->xb', phi, third, preferred_element_type=jnp.float32)  36.3 us
    another operation x2, local copies, waits for them, and re-layouts, sink_side(): sink_elem[:, local, group * span:(group + 1) * span]  26.9 us
    gather x2, local copies, waits for them, and re-layouts, on_device(): chosen = jnp.take(source, other, axis=1)  26.2 us
  transfers between devices with their start and end apart: 3, of which 2 were waited for; matrix products, arithmetic and copies ran while one was open for 31% of the time, Pallas kernels for 0%

profile of v1, /device:TPU:0, one launch (start us, length us, event | category | flops | bytes accessed | tf_op | source)
XLA Modules:
  0.0 1050.1 jit_solution(15477032726458004033)
XLA Ops:
  20.9 11.6 %fusion.102 = (bf16[2,1,128,16384]{3,2,1,0:T(8,128)(2,1)}, bf16[2,1,128,16384]{3,2,1,0:T(8,128)(2,1)}) fusion(bf16[2,1,256,16384]{3,2,1,0:T(8,128)(2,1)} %param.7), kind=kLoop, calls=%fused_computation.200 | loop fusion | bytes 33554432 | tf_op jit(solution)/shard_map/slice | solution.py:39
  32.5 13.5 %reshape_squeeze.21 = bf16[2,16384,128]{2,1,0:T(8,128)(2,1)} reshape(bf16[2,1,128,16384]{3,2,1,0:T(8,128)(2,1)} %get-tuple-element.32) | data formatting | bytes 16777216 | tf_op jit(solution)/shard_map/reshape;squeeze | solution.py:39
  45.9 13.5 %reshape_squeeze.22 = bf16[2,16384,128]{2,1,0:T(8,128)(2,1)} reshape(bf16[2,1,128,16384]{3,2,1,0:T(8,128)(2,1)} %get-tuple-element.33) | data formatting | bytes 16777216 | tf_op jit(solution)/shard_map/reshape;squeeze | solution.py:39
  70.7 9.2 fusion.33
  79.9 9.2 copy.85
  89.1 26.0 %fusion.18 = bf16[128,256,128]{2,1,0:T(8,128)(2,1)} fusion(bf16[128,128,2,128]{1,0,3,2:T(8,128)(2,1)} %bitcast.406, bf16[1,128,256]{1,2,0:T(8,128)(2,1)S(1)} %get-tuple-element.57, bf16[1,128,256]{1,2,0:T(8,128)(2,1)S(1)} %get-tuple-element.56), kind=kOutput, calls=%fused_computation.45 | convolution fusion | flops 2151940096 | bytes 16908288 | tf_op jit(solution)/shard_map/ijck,cjb->ibk/dot_general | solution.py:42
  115.1 12.7 %reshape.129 = bf16[128,2,16384]{2,1,0:T(2,128)(2,1)} reshape(bf16[128,256,128]{2,1,0:T(8,128)(2,1)} %fusion.18) | data formatting | bytes 16777216 | tf_op jit(solution)/shard_map/reshape | solution.py:43
  127.8 12.0 %copy.125 = bf16[128,2,16384]{2,0,1:T(8,128)(2,1)} copy(bf16[128,2,16384]{2,1,0:T(2,128)(2,1)} %reshape.129) | data formatting | bytes 16777216 | tf_op jit(solution)/shard_map/reshape | solution.py:43
  139.8 9.0 fusion.32
  148.8 9.2 copy.86
  158.0 25.8 %fusion.21 = bf16[128,256,128]{2,1,0:T(8,128)(2,1)} fusion(bf16[128,128,2,128]{1,0,3,2:T(8,128)(2,1)} %bitcast.404, bf16[1,128,256]{1,2,0:T(8,128)(2,1)S(1)} %get-tuple-element.61, bf16[1,128,256]{1,2,0:T(8,128)(2,1)S(1)} %get-tuple-element.60), kind=kOutput, calls=%fused_computation.46 | convolution fusion | flops 2151940096 | bytes 16908288 | tf_op jit(solution)/shard_map/ijck,cjb->ibk/dot_general | solution.py:42
  183.8 12.9 %reshape.131 = bf16[128,2,16384]{2,1,0:T(2,128)(2,1)} reshape(bf16[128,256,128]{2,1,0:T(8,128)(2,1)} %fusion.21) | data formatting | bytes 16777216 | tf_op jit(solution)/shard_map/reshape | solution.py:43
  196.7 12.0 %copy.124 = bf16[128,2,16384]{2,0,1:T(8,128)(2,1)} copy(bf16[128,2,16384]{2,1,0:T(2,128)(2,1)} %reshape.131) | data formatting | bytes 16777216 | tf_op jit(solution)/shard_map/reshape | solution.py:43
  238.8 9.0 fusion.31
  247.8 9.2 copy.87
  257.0 25.8 %fusion.24 = bf16[128,256,128]{2,1,0:T(8,128)(2,1)} fusion(bf16[128,128,2,128]{1,0,3,2:T(8,128)(2,1)} %bitcast.407, bf16[1,128,256]{1,2,0:T(8,128)(2,1)S(1)} %get-tuple-element.65, bf16[1,128,256]{1,2,0:T(8,128)(2,1)S(1)} %get-tuple-element.64), kind=kOutput, calls=%fused_computation.47 | convolution fusion | flops 2151940096 | bytes 16908288 | tf_op jit(solution)/shard_map/ijck,cjb->ibk/dot_general | solution.py:42
  282.8 12.7 %reshape.134 = bf16[128,2,16384]{2,1,0:T(2,128)(2,1)} reshape(bf16[128,256,128]{2,1,0:T(8,128)(2,1)} %fusion.24) | data formatting | bytes 16777216 | tf_op jit(solution)/shard_map/reshape | solution.py:43
  295.5 11.9 %copy.123 = bf16[128,2,16384]{2,0,1:T(8,128)(2,1)} copy(bf16[128,2,16384]{2,1,0:T(2,128)(2,1)} %reshape.134) | data formatting | bytes 16777216 | tf_op jit(solution)/shard_map/reshape | solution.py:43
  307.4 9.0 fusion.30
  316.4 9.2 copy.88
  325.7 26.0 %fusion.27 = bf16[128,256,128]{2,1,0:T(8,128)(2,1)} fusion(bf16[128,128,2,128]{1,0,3,2:T(8,128)(2,1)} %bitcast.405, bf16[1,128,256]{1,2,0:T(8,128)(2,1)S(1)} %get-tuple-element.69, bf16[1,128,256]{1,2,0:T(8,128)(2,1)S(1)} %get-tuple-element.68), kind=kOutput, calls=%fused_computation.48 | convolution fusion | flops 2151940096 | bytes 16908288 | tf_op jit(solution)/shard_map/ijck,cjb->ibk/dot_general | solution.py:42
  351.7 12.7 %reshape.136 = bf16[128,2,16384]{2,1,0:T(2,128)(2,1)} reshape(bf16[128,256,128]{2,1,0:T(8,128)(2,1)} %fusion.27) | data formatting | bytes 16777216 | tf_op jit(solution)/shard_map/reshape | solution.py:43
  364.3 12.0 %copy.122 = bf16[128,2,16384]{2,0,1:T(8,128)(2,1)} copy(bf16[128,2,16384]{2,1,0:T(2,128)(2,1)} %reshape.136) | data formatting | bytes 16777216 | tf_op jit(solution)/shard_map/reshape | solution.py:43
  397.3 202.7 %all-to-all-done = bf16[8,2,1,256,2048]{4,3,2,1,0:T(8,128)(2,1)} async-done(((bf16[8,2,1,256,2048]{4,3,2,1,0:T(8,128)(2,1)}), bf16[8,2,1,256,2048]{4,3,2,1,0:T(8,128)(2,1)}, u32[]{:S(2)}, u32[]{:S(2)}) %all-to-all-start) | async-done | bytes 16777248 | tf_op jit(solution)/shard_map/all_to_all | solution.py:52
  605.9 23.5 %fusion.99 = (bf16[2,1,2048,2048]{3,2,1,0:T(8,128)(2,1)}, bf16[2,1,2048,2048]{3,2,1,0:T(8,128)(2,1)}) fusion(bf16[2,2,2048,2048]{3,2,1,0:T(8,128)(2,1)} %param.8), kind=kLoop, calls=%fused_computation.197 | loop fusion | bytes 67108864 | tf_op jit(solution)/shard_map/slice | solution.py:58
  629.4 13.1 %gather_fusion.3 = bf16[16,2,128,2048]{3,2,1,0:T(8,128)(2,1)} fusion(bf16[2,16,128,2048]{3,2,1,0:T(8,128)(2,1)} %bitcast.403, s32[1024]{0:T(1024)S(1)} %pad_clamp_fusion), kind=kCustom, calls=%fused_computation.clone | custom fusion | bytes 33554496 | tf_op jit(solution)/shard_map/jit(_take)/gather | solution.py:59
  642.5 13.1 %gather_fusion.4 = bf16[16,2,128,2048]{3,2,1,0:T(8,128)(2,1)} fusion(bf16[2,16,128,2048]{3,2,1,0:T(8,128)(2,1)} %bitcast.402, s32[1024]{0:T(1024)S(1)} %pad_clamp_fusion), kind=kCustom, calls=%fused_computation.1.clone | custom fusion | bytes 33554496 | tf_op jit(solution)/shard_map/jit(_take)/gather | solution.py:59
  656.4 23.2 %fusion.5 = (bf16[2,16,128,2048]{3,2,1,0:T(8,128)(2,1)}, bf16[2,16,128,2048]{3,2,1,0:T(8,128)(2,1)}) fusion(bf16[16,2,128,2048]{3,2,1,0:T(8,128)(2,1)} %gather_fusion.3, pred[16]{0:T(512)(128)(4,1)S(1)} %compare_and_fusion, bf16[16,2,128,2048]{3,2,1,0:T(8,128)(2,1)} %gather_fusion.4), kind=kLoop, calls=%fused_computation.23 | loop fusion | flops 16777216 | bytes 67108880 | tf_op jit(solution)/shard_map/jit(_take)/select_n | solution.py:59
  700.9 12.1 %fusion.10 = f32[16,128,128]{2,1,0:T(8,128)} fusion(bf16[16,128,2048]{2,1,0:T(8,128)(2,1)} %bitcast.418, bf16[2,16,128,2048]{3,2,1,0:T(8,128)(2,1)} %get-tuple-element.84), kind=kOutput, calls=%fused_computation.37 | convolution fusion | flops 1073741824 | bytes 17825792 | tf_op jit(solution)/shard_map/oic,ojc->oij/dot_general | solution.py:63
  726.9 242.6 %all-to-all-done.1 = bf16[8,2,1,256,2048]{4,3,2,1,0:T(8,128)(2,1)} async-done(((bf16[8,2,1,256,2048]{4,3,2,1,0:T(8,128)(2,1)}), bf16[8,2,1,256,2048]{4,3,2,1,0:T(8,128)(2,1)}, u32[]{:S(2)}, u32[]{:S(2)}) %all-to-all-start.1) | async-done | bytes 16777248 | tf_op jit(solution)/shard_map/all_to_all | solution.py:52
  982.5 12.1 %fusion.14 = f32[16,128,128]{2,1,0:T(8,128)} fusion(bf16[16,128,2048]{2,1,0:T(8,128)(2,1)} %bitcast.416, bf16[2,16,128,2048]{3,2,1,0:T(8,128)(2,1)} %get-tuple-element.85), kind=kOutput, calls=%fused_computation.41 | convolution fusion | flops 1073741824 | bytes 17825792 | tf_op jit(solution)/shard_map/oic,ojc->oij/dot_general | solution.py:63
  1027.8 14.5 %psum.7 = f32[2,1,2,16,1]{3,2,0,4,1:T(2,128)S(1)} all-reduce(f32[2,1,2,16,1]{3,2,0,4,1:T(2,128)S(1)} %bitcast.422), channel_id=1, replica_groups=mesh['tm'=4,'op'=8] {'op'}, use_global_device_ids=true, to_apply=%region_4.6 | all-reduce | flops 64 | bytes 512 | tf_op jit(solution)/shard_map/psum | solution.py:79
  (88 shorter events, 156.2 us)
Async XLA Ops:
  6.5 52.9 %all-gather.2.cloned.1.call-start = ((), (), s32[]{:S(2)}) async-start(), calls=%async_computation.2 | async-start | bytes 2359296 | tf_op jit(solution)/shard_map/all_gather | solution.py:20
  70.5 9.4 copy-start.3
  229.7 370.3 %all-to-all-start = ((bf16[8,2,1,256,2048]{4,3,2,1,0:T(8,128)(2,1)}), bf16[8,2,1,256,2048]{4,3,2,1,0:T(8,128)(2,1)}, u32[]{:S(2)}, u32[]{:S(2)}) async-start(bf16[8,2,1,256,2048]{4,3,2,1,0:T(8,128)(2,1)} %fusion.42), calls=%async_computation | async-start | bytes 33554432 | tf_op jit(solution)/shard_map/all_to_all | solution.py:52
  397.3 208.6 %copy-start.7 = (s32[16,1]{0,1:T(1,128)S(1)}, s32[16,1]{0,1:T(1,128)}, u32[]{:S(2)}) copy-start(s32[16,1]{0,1:T(1,128)} %param.10) | copy-start | bytes 196
  600.0 369.6 %all-to-all-start.1 = ((bf16[8,2,1,256,2048]{4,3,2,1,0:T(8,128)(2,1)}), bf16[8,2,1,256,2048]{4,3,2,1,0:T(8,128)(2,1)}, u32[]{:S(2)}, u32[]{:S(2)}) async-start(bf16[8,2,1,256,2048]{4,3,2,1,0:T(8,128)(2,1)} %fusion.34), calls=%async_computation.1 | async-start | bytes 33554432 | tf_op jit(solution)/shard_map/all_to_all | solution.py:52
  642.5 13.1 %copy-start = (s32[16,3]{0,1:T(4,128)S(1)}, s32[16,3]{0,1:T(4,128)}, u32[]{:S(2)}) copy-start(s32[16,3]{0,1:T(4,128)} %param.11) | copy-start | bytes 580
  656.4 23.2 %copy-start.4 = (bf16[2,1,1,512,512]{3,4,2,1,0:T(8,128)(2,1)S(1)}, bf16[2,1,1,512,512]{3,4,2,1,0:T(8,128)(2,1)}, u32[]{:S(2)}) copy-start(bf16[2,1,1,512,512]{3,4,2,1,0:T(8,128)(2,1)} %copy-done.3) | copy-start | bytes 3145732
  700.9 12.1 %copy-start.1 = (bf16[1,1,8,256,2048]{4,3,2,1,0:T(8,128)(2,1)}, bf16[1,1,8,256,2048]{4,3,2,1,0:T(8,128)(2,1)S(1)}, u32[]{:S(2)}) copy-start(bf16[1,1,8,256,2048]{4,3,2,1,0:T(8,128)(2,1)S(1)} %get-tuple-element.28) | copy-start | bytes 25165828
  982.5 12.1 %copy-start.2 = (bf16[1,1,8,256,2048]{4,3,2,1,0:T(8,128)(2,1)}, bf16[1,1,8,256,2048]{4,3,2,1,0:T(8,128)(2,1)S(1)}, u32[]{:S(2)}) copy-start(bf16[1,1,8,256,2048]{4,3,2,1,0:T(8,128)(2,1)S(1)} %get-tuple-element.30) | copy-start | bytes 25165828
  1001.3 8.5 copy-start.6
  1009.8 9.0 copy-start.5
Sparse Core Ops, SparseCore 0:
  8.9 31.8 all-gather.1
